TPU v7x, 512 devices: a whole 4x4x16 slice. The times are simulated.
512 devices in a mesh: subj: 32 (over y, z_lo), slab: 16 (over x, z_hi, core).
Axes of the slice: x: 4, y: 4, z: 16 (z_hi: 2, z_lo: 8; z = z_hi * 8 + z_lo), core: 2. Of those that a mesh axis runs over, the one named last changes fastest.
Arguments:
- image: float32 [32, 192, 32, 192], P('subj', 'slab'), may hold values from -6 to 6
- velocity: float32 [32, 3, 192, 32, 192], P('subj', None, 'slab'), may hold values from -3 to 3
- template: float32 [192, 32, 192], P('slab', 'subj'), may hold values from -6 to 6
- z_kernel: float32 [192, 192], replicated, as said below
- x_kernel: float32 [192, 192], replicated, as said below
Outputs:
- velocity_update: float32 [32, 3, 192, 32, 192], P('subj', None, 'slab')
- new_template: float32 [192, 32, 192], P('slab', 'subj')
Inputs may be any that keep to these rules, and one draw needn't show every extreme that they name: `z_kernel`: entries are positive. `x_kernel`: entries are positive.
All inputs are finite; a program needn't handle non-finite values.
Results may differ from a plain program's by a relative error of at most 0.00028.
Values sent between devices are 32-bit elements; how exact they have to be, the bound alone decides.
No kernel may reach another device: no remote copies, remote signals or barrier semaphores. Data moves between devices by JAX's collectives and lax.ppermute only.
A program may use at most 64 MiB of HBM per device.

v0:
```python
import jax
import jax.numpy as jnp
from jax import lax
from jax.sharding import PartitionSpec as P


def with_halo(x, sides, width):
    for axis, dim in sides:
        size, length = (lax.axis_size(axis), x.shape[dim])
        up = [(i, (i + 1) % size) for i in range(size - 1)]
        down = [(j, i) for i, j in up]
        last = lax.slice_in_dim(x, length - width, length, axis=dim)
        leading = lax.slice_in_dim(x, 0, width, axis=dim)
        before = lax.ppermute(last, axis, up)
        after = lax.ppermute(leading, axis, down)
        x = jnp.concatenate([before, x, after], axis=dim)
    return x


def gradients(padded):
    slope_z = (padded[2:, 1:-1, 1:-1] - padded[:-2, 1:-1, 1:-1]) * 0.5
    slope_y = (padded[1:-1, 2:, 1:-1] - padded[1:-1, :-2, 1:-1]) * 0.5
    slope_x = (padded[1:-1, 1:-1, 2:] - padded[1:-1, 1:-1, :-2]) * 0.5
    return jnp.stack([slope_z, slope_y, slope_x])


def per_device(image, velocity, template, z_kernel, x_kernel):
    highest = lax.Precision.HIGHEST
    full_rows = lax.all_gather(template, "subj", axis=1, tiled=True)
    with_rims = with_halo(full_rows, (("slab", 0),), 1)
    padded = jnp.pad(with_rims, ((0, 0), (1, 1), (1, 1)))
    slopes = gradients(padded)
    warped = full_rows[None] + jnp.sum(velocity * slopes[None], 1)
    residual = image - warped
    forces = residual[:, None] * slopes[None]
    along_x = jnp.einsum("sczyx,wx->sczyw", forces, x_kernel, precision=highest)
    along_z = jnp.einsum(
        "vz,sczyx->scvyx",
        z_kernel,
        lax.all_to_all(along_x, "slab", split_axis=3, concat_axis=2, tiled=True),
        precision=highest,
    )
    velocity_update = lax.all_to_all(along_z, "slab", split_axis=2, concat_axis=3, tiled=True)
    local_sum = jnp.sum(residual, 0)
    subjects = lax.axis_size("subj") * image.shape[0]
    summed = lax.psum_scatter(local_sum, "subj", scatter_dimension=1, tiled=True)
    new_template = template + summed / subjects
    return (velocity_update, new_template)


def solution(mesh):
    in_specs = (
        P("subj", "slab", None, None),
        P("subj", None, "slab", None, None),
        P("slab", "subj", None),
        P(),
        P(),
    )
    out_specs = (P("subj", None, "slab", None, None), P("slab", "subj", None))
    return jax.shard_map(
        per_device, mesh=mesh, in_specs=in_specs, out_specs=out_specs, check_vma=False
    )
```

profile of v0, /device:TPU:4, one launch (start us, length us, event | category | flops | bytes accessed | tf_op | source)
XLA Modules:
  0.0 502.2 jit_solution(7305345701270509311)
XLA Ops:
  7.2 0.8 copy.43
  7.9 130.0 %all_gather.3 = f32[12,32,192]{2,0,1:T(8,128)S(1)} all-gather(f32[12,1,192]{2,0,1:T(8,128)S(1)} %copy.43), channel_id=1, replica_groups=mesh['subj'=32,'slab'=16] {'subj'}, dimensions={1}, use_global_device_ids=true | all-gather | bytes 304128 | tf_op jit(solution)/shard_map/all_gather | solution.py:29
  138.0 1.9 collective-permute-start.1
  139.9 13.3 %collective-permute-start = (f32[1,32,192]{2,0,1:T(1,128)S(1)}, f32[1,32,192]{2,0,1:T(1,128)S(1)}, u32[]{:S(2)}, u32[]{:S(2)}) collective-permute-start(f32[1,32,192]{2,0,1:T(1,128)S(1)} %get-tuple-element.13), channel_id=1, source_target_pairs={{1,0},{2,1},{3,2},{4,3},{5,4},{6,5},{7,6},{8,7},{9,8},{10,9},{11,1... | collective-permute-start | bytes 73736 | tf_op jit(solution)/shard_map/ppermute | solution.py:15
  153.2 1.6 collective-permute-done
  155.1 0.6 fusion.10
  155.7 0.6 copy-done.2
  156.3 1.0 fusion
  158.0 0.5 copy-done.1
  158.5 1.7 convolution_bitcast_fusion.1
  160.2 1.2 copy.47
  161.4 70.8 %all_to_all.33 = f32[1,3,12,32,192]{4,0,2,1,3:T(1,128)S(1)} all-to-all(f32[1,3,12,32,192]{4,0,2,1,3:T(1,128)S(1)} %copy.47), channel_id=1, replica_groups=mesh['subj'=32,'slab'=16] {'slab'}, dimensions={3} | all-to-all | bytes 1769472 | tf_op jit(solution)/shard_map/all_to_all | solution.py:40
  232.3 1.3 copy.48
  233.6 0.6 copy.49
  234.5 2.3 convolution_bitcast_fusion
  236.8 1.5 copy.51
  238.4 8.6 %all-to-all-start.1 = ((f32[1,3,192,2,192]{4,3,1,0,2:T(2,128)}), f32[1,3,192,2,192]{4,3,1,0,2:T(2,128)S(1)}, u32[]{:S(2)}, u32[]{:S(2)}) async-start(f32[1,3,192,2,192]{4,3,1,0,2:T(2,128)} %copy.51), calls=%async_computation.1 | async-start | bytes 2359296 | tf_op jit(solution)/shard_map/all_to_all | solution.py:43
  247.0 0.7 reduce-scatter.2.cloned.1.call-update
  247.6 243.6 %reduce-scatter.2.cloned.1.call-done = f32[12,1,192]{2,0,1:T(8,128)} async-done(((f32[12,32,192]{2,0,1:T(8,128)}), f32[12,1,192]{2,0,1:T(8,128)}) %reduce-scatter.2.cloned.1.call-update) | async-done | bytes 9232 | tf_op jit(solution)/shard_map/reduce_scatter | solution.py:46
  491.3 0.7 multiply_add_fusion
  492.0 0.6 copy.56
  492.6 0.4 copy.52
  493.0 1.2 copy.53
  494.2 1.1 copy.55
  (17 shorter events, 1.3 us)
Async XLA Ops:
  7.2 151.3 %copy-start = (f32[192,192]{1,0:T(8,128)S(1)}, f32[192,192]{1,0:T(8,128)}, u32[]{:S(2)}) copy-start(f32[192,192]{1,0:T(8,128)} %param.9) | copy-start | bytes 442372
  138.0 15.2 %collective-permute-start.1 = (f32[1,32,192]{2,0,1:T(1,128)S(1)}, f32[1,32,192]{2,0,1:T(1,128)S(1)}, u32[]{:S(2)}, u32[]{:S(2)}) collective-permute-start(f32[1,32,192]{2,0,1:T(1,128)S(1)} %get-tuple-element.12), channel_id=1, source_target_pairs={{0,1},{1,2},{2,3},{3,4},{4,5},{5,6},{6,7},{7,8},{8,9},{9,10},{10,1... | collective-permute-start | bytes 73736 | tf_op jit(solution)/shard_map/ppermute | solution.py:14
  139.9 14.8 %collective-permute-start = (f32[1,32,192]{2,0,1:T(1,128)S(1)}, f32[1,32,192]{2,0,1:T(1,128)S(1)}, u32[]{:S(2)}, u32[]{:S(2)}) collective-permute-start(f32[1,32,192]{2,0,1:T(1,128)S(1)} %get-tuple-element.13), channel_id=1, source_target_pairs={{1,0},{2,1},{3,2},{4,3},{5,4},{6,5},{7,6},{8,7},{9,8},{10,9},{11,1... | collective-permute-start | bytes 73736 | tf_op jit(solution)/shard_map/ppermute | solution.py:15
  155.1 1.3 copy-start.2
  156.3 1.1 copy-start.3
  157.7 0.8 copy-start.1
  233.6 0.9 copy-start.4
  238.4 252.9 %copy-start.5 = (f32[12,1,192]{2,1,0:T(1,128)S(1)}, f32[12,1,192]{2,1,0:T(1,128)}, u32[]{:S(2)}) copy-start(f32[12,1,192]{2,1,0:T(1,128)} %param.7) | copy-start | bytes 27652
  238.4 254.3 %all-to-all-start.1 = ((f32[1,3,192,2,192]{4,3,1,0,2:T(2,128)}), f32[1,3,192,2,192]{4,3,1,0,2:T(2,128)S(1)}, u32[]{:S(2)}, u32[]{:S(2)}) async-start(f32[1,3,192,2,192]{4,3,1,0,2:T(2,128)} %copy.51), calls=%async_computation.1 | async-start | bytes 2359296 | tf_op jit(solution)/shard_map/all_to_all | solution.py:43
  246.9 244.4 %reduce-scatter.2.cloned.1.call-start = ((), (), s32[]{:S(2)}) async-start(), calls=%async_computation.3 | async-start | bytes 540672 | tf_op jit(solution)/shard_map/reduce_scatter | solution.py:46
Sparse Core Ops, SparseCore 0:
  250.5 240.7 reduce-scatter.1
where the time goes:
time: 503 us; the launch traced here: 502 us
  waiting for transfers between devices  246 us (49%)
  blocking collectives  201 us (40%)
  starting transfers between devices  23.8 us (5%)
  between operations  14.2 us (3%)
  local copies, waits for them, and re-layouts  10.3 us (2%)
    reduce_scatter x1, waiting for transfers between devices, per_device(): lax.psum_scatter(local_sum, 'subj', scatter_dimension=1, tiled=True)  244 us
    all_gather x1, blocking collectives, per_device(): full_rows = lax.all_gather(template, 'subj', axis=1, tiled=True)  130 us
    all_to_all x1, blocking collectives, per_device(): lax.all_to_all(along_x, 'slab', split_axis=3, concat_axis=2, tiled=True)  70.8 us
    ppermute x1, starting transfers between devices, with_halo(): after = lax.ppermute(leading, axis, down)  13.3 us
  transfers between devices with their start and end apart: 4, of which 2 were waited for; matrix products, arithmetic and copies ran while one was open for 0% of the time, Pallas kernels for 0%

commit v1 on v0

--- a/solution.py
+++ b/solution.py
@@ -26,7 +26,9 @@
 
 def per_device(image, velocity, template, z_kernel, x_kernel):
     highest = lax.Precision.HIGHEST
-    full_rows = lax.all_gather(template, "subj", axis=1, tiled=True)
+    full_rows = jnp.concatenate(
+        lax.all_to_all(jnp.stack([template] * lax.axis_size("subj")), "subj", 0, 0), axis=1
+    )
     with_rims = with_halo(full_rows, (("slab", 0),), 1)
     padded = jnp.pad(with_rims, ((0, 0), (1, 1), (1, 1)))
     slopes = gradients(padded)

time: 503 us -> 422 us (0.84)
  blocking collectives: 201 us -> 106 us
  waiting for transfers between devices: 246 us -> 259 us
    all_gather x1 -> x0, blocking collectives: 130 us -> none  [per_device(): full_rows = lax.all_gather(template, 'subj', axis=1, tiled=True)]
    all_to_all x0 -> x1, blocking collectives: none -> 40.2 us  [per_device(): lax.all_to_all(jnp.stack([template] * lax.axis_size('subj')), 'subj', 0, 0)]
    reduce_scatter x1, waiting for transfers between devices: 244 us -> 257 us  [per_device(): lax.psum_scatter(local_sum, 'subj', scatter_dimension=1, tiled=True)]
  transfers between devices with their start and end apart: 4 -> 4, of which waited for: 2 -> 2; matrix products, arithmetic and copies ran while one was open for 0% -> 1% of each run, Pallas kernels for 0% -> 0%
where the time goes in v1:
time: 422 us; the launch traced here: 421 us
  waiting for transfers between devices  259 us (61%)
  blocking collectives  106 us (25%)
  starting transfers between devices  24.6 us (6%)
  between operations  14.2 us (3%)
  local copies, waits for them, and re-layouts  12 us (3%)
    reduce_scatter x1, waiting for transfers between devices, per_device(): lax.psum_scatter(local_sum, 'subj', scatter_dimension=1, tiled=True)  257 us
    all_to_all x1, blocking collectives, per_device(): lax.all_to_all(along_x, 'slab', split_axis=3, concat_axis=2, tiled=True)  66.2 us
    all_to_all x1, blocking collectives, per_device(): lax.all_to_all(jnp.stack([template] * lax.axis_size('subj')), 'subj', 0, 0)  40.2 us
    ppermute x1, starting transfers between devices, with_halo(): after = lax.ppermute(leading, axis, down)  13.3 us
    all_to_all x1, starting transfers between devices, per_device(): lax.all_to_all(along_z, 'slab', split_axis=2, concat_axis=3, tiled=True)  9.39 us
  transfers between devices with their start and end apart: 4, of which 2 were waited for; matrix products, arithmetic and copies ran while one was open for 1% of the time, Pallas kernels for 0%

profile of v1, /device:TPU:4, one launch (start us, length us, event | category | flops | bytes accessed | tf_op | source)
XLA Modules:
  0.0 421.4 jit_solution(9024128651024589568)
XLA Ops:
  7.2 0.8 copy.64
  8.1 40.2 %all_to_all.38 = f32[32,12,1,192]{3,2,1,0:T(1,128)S(1)} all-to-all(f32[32,12,1,192]{3,2,1,0:T(1,128)S(1)} %stack.10), channel_id=1, replica_groups=mesh['subj'=32,'slab'=16] {'subj'}, dimensions={0} | all-to-all | bytes 589824 | tf_op jit(solution)/shard_map/all_to_all | solution.py:30
  48.4 1.9 collective-permute-start.1
  50.4 13.3 %collective-permute-start = (f32[1,32,192]{2,1,0:T(8,128)S(1)}, f32[1,32,192]{2,1,0:T(8,128)S(1)}, u32[]{:S(2)}, u32[]{:S(2)}) collective-permute-start(f32[1,32,192]{2,1,0:T(8,128)S(1)} %get-tuple-element.13), channel_id=1, source_target_pairs={{1,0},{2,1},{3,2},{4,3},{5,4},{6,5},{7,6},{8,7},{9,8},{10,9},{11,1... | collective-permute-start | bytes 73736 | tf_op jit(solution)/shard_map/ppermute | solution.py:15
  63.6 1.6 collective-permute-done
  65.4 0.4 fusion.10
  65.8 0.9 copy-done.1
  67.0 0.7 copy-done.2
  67.8 1.1 convolution_bitcast_fusion.1
  69.0 1.2 copy.42
  70.2 66.2 %all_to_all.39 = f32[1,3,12,32,192]{4,0,2,1,3:T(1,128)S(1)} all-to-all(f32[1,3,12,32,192]{4,0,2,1,3:T(1,128)S(1)} %copy.42), channel_id=1, replica_groups=mesh['subj'=32,'slab'=16] {'slab'}, dimensions={3} | all-to-all | bytes 1769472 | tf_op jit(solution)/shard_map/all_to_all | solution.py:42
  136.4 1.3 copy.43
  137.7 0.6 copy.44
  138.4 0.3 copy-done.3
  138.7 2.3 convolution_bitcast_fusion
  141.0 1.5 copy.46
  142.5 9.4 %all-to-all-start.2 = ((f32[1,3,192,2,192]{4,3,1,0,2:T(2,128)}), f32[1,3,192,2,192]{4,3,1,0,2:T(2,128)S(1)}, u32[]{:S(2)}, u32[]{:S(2)}) async-start(f32[1,3,192,2,192]{4,3,1,0,2:T(2,128)} %copy.46), calls=%async_computation.2 | async-start | bytes 2359296 | tf_op jit(solution)/shard_map/all_to_all | solution.py:45
  152.0 1.0 copy.49
  153.0 257.5 %reduce-scatter.2.cloned.1.call-done = f32[12,1,192]{2,0,1:T(8,128)} async-done(((f32[12,32,192]{2,0,1:T(8,128)}), f32[12,1,192]{2,0,1:T(8,128)}) %reduce-scatter.2.cloned.1.call-update) | async-done | bytes 9232 | tf_op jit(solution)/shard_map/reduce_scatter | solution.py:48
  410.5 0.7 copy_add_fusion
  411.2 0.6 copy.52
  411.8 0.4 copy.47
  412.2 1.2 copy.48
  413.4 1.1 copy.51
  (17 shorter events, 1.0 us)
Async XLA Ops:
  7.2 60.7 %copy-start = (f32[192,192]{1,0:T(8,128)S(1)}, f32[192,192]{1,0:T(8,128)}, u32[]{:S(2)}) copy-start(f32[192,192]{1,0:T(8,128)} %param.9) | copy-start | bytes 442372
  48.4 15.2 %collective-permute-start.1 = (f32[1,32,192]{2,1,0:T(8,128)S(1)}, f32[1,32,192]{2,1,0:T(8,128)S(1)}, u32[]{:S(2)}, u32[]{:S(2)}) collective-permute-start(f32[1,32,192]{2,1,0:T(8,128)S(1)} %get-tuple-element.12), channel_id=1, source_target_pairs={{0,1},{1,2},{2,3},{3,4},{4,5},{5,6},{6,7},{7,8},{8,9},{9,10},{10,1... | collective-permute-start | bytes 73736 | tf_op jit(solution)/shard_map/ppermute | solution.py:14
  50.4 14.8 %collective-permute-start = (f32[1,32,192]{2,1,0:T(8,128)S(1)}, f32[1,32,192]{2,1,0:T(8,128)S(1)}, u32[]{:S(2)}, u32[]{:S(2)}) collective-permute-start(f32[1,32,192]{2,1,0:T(8,128)S(1)} %get-tuple-element.13), channel_id=1, source_target_pairs={{1,0},{2,1},{3,2},{4,3},{5,4},{6,5},{7,6},{8,7},{9,8},{10,9},{11,1... | collective-permute-start | bytes 73736 | tf_op jit(solution)/shard_map/ppermute | solution.py:15
  65.4 1.3 copy-start.1
  66.7 1.0 copy-start.2
  137.7 0.9 copy-start.3
  142.5 269.3 %all-to-all-start.2 = ((f32[1,3,192,2,192]{4,3,1,0,2:T(2,128)}), f32[1,3,192,2,192]{4,3,1,0,2:T(2,128)S(1)}, u32[]{:S(2)}, u32[]{:S(2)}) async-start(f32[1,3,192,2,192]{4,3,1,0,2:T(2,128)} %copy.46), calls=%async_computation.2 | async-start | bytes 2359296 | tf_op jit(solution)/shard_map/all_to_all | solution.py:45
  151.9 258.6 %copy-start.4 = (f32[12,1,192]{2,1,0:T(1,128)S(1)}, f32[12,1,192]{2,1,0:T(1,128)}, u32[]{:S(2)}) copy-start(f32[12,1,192]{2,1,0:T(1,128)} %param.7) | copy-start | bytes 27652
  151.9 258.6 %reduce-scatter.2.cloned.1.call-start = ((), (), s32[]{:S(2)}) async-start(), calls=%async_computation.4 | async-start | bytes 540672 | tf_op jit(solution)/shard_map/reduce_scatter | solution.py:48
Sparse Core Ops, SparseCore 0:
  155.5 254.8 reduce-scatter.1
